TPU v7x, 512 devices: a whole 4x4x16 slice. The times are simulated.
512 devices in a mesh: blk: 128 (over z_lo, y, x), off: 4 (over z_hi, core).
Axes of the slice: x: 4, y: 4, z: 16 (z_hi: 2, z_lo: 8; z = z_hi * 8 + z_lo), core: 2. Of those that a mesh axis runs over, the one named last changes fastest.
Arguments:
- coefficients: bfloat16 [2048, 32, 128], P('blk', 'off'), may hold values from -12 to 12
Outputs:
- smoothed: float32 [2048, 32, 128], P(('blk', 'off'))
- log_degree: float32 [2048], P(('blk', 'off'))
All inputs are finite; a program needn't handle non-finite values.
Results may differ from a plain program's by a relative error of at most 0.005.
Values may be sent and summed in bfloat16 or wider, within the bound.
A program may use at most 64 MiB of HBM per device.

v0:
```python
import math
import jax
import jax.numpy as jnp
from jax import lax
from jax.sharding import PartitionSpec as P

epsilon = 1e-06
concentration = 40.0


def shifted(array, axis, by):
    count = lax.axis_size(axis)
    return lax.ppermute(array, axis, [(i, (i + by) % count) for i in range(count)])


def angle_tables(angular):
    half_width = angular // 2
    frequency = jnp.arange(half_width, dtype=jnp.int32)
    shifts = jnp.arange(angular, dtype=jnp.int32)
    product = frequency[:, None] * shifts[None, :] % angular
    phase = product.astype(jnp.float32) * (2.0 * math.pi / angular)
    forward = jnp.concatenate([jnp.cos(phase), -jnp.sin(phase)], axis=0)
    return (forward, forward.T)


def inverse_norms(block_values):
    values = block_values.astype(jnp.float32)
    return lax.rsqrt(jnp.sum(values * values, axis=(1, 2)) + epsilon)


def tile_terms(own_block, own_inverse, other_block, offset, forward, backward):
    row_count = own_block.shape[0]
    half_width = own_block.shape[2] // 2
    highest = lax.Precision.HIGHEST
    other_inverse = inverse_norms(other_block)
    swapped = jnp.concatenate(
        [other_block[:, :, half_width:], other_block[:, :, :half_width]], axis=2
    )
    direct = jnp.einsum("irc,jrc->ijc", own_block, other_block, preferred_element_type=jnp.float32)
    mixed_terms = jnp.einsum("irc,jrc->ijc", own_block, swapped, preferred_element_type=jnp.float32)
    real_part = direct[:, :, :half_width] + direct[:, :, half_width:]
    imag_part = mixed_terms[:, :, half_width:] - mixed_terms[:, :, :half_width]
    cross_spectrum = jnp.concatenate([real_part, imag_part], axis=2).reshape(
        row_count * row_count, -1
    )
    correlation = jnp.dot(
        cross_spectrum, forward, precision=highest, preferred_element_type=jnp.float32
    )
    correlation = correlation.reshape(row_count, row_count, -1)
    cosine = correlation * own_inverse[:, None, None] * other_inverse[None, :, None]
    same_image = jnp.arange(row_count)[:, None] == jnp.arange(row_count)[None, :]
    keep_mask = jnp.where(jnp.logical_and(offset == 0, same_image), 0.0, 1.0).astype(jnp.float32)
    weights = jnp.exp(concentration * cosine) * keep_mask[:, :, None]
    spectral = jnp.dot(
        weights.reshape(row_count * row_count, -1),
        backward,
        precision=highest,
        preferred_element_type=jnp.float32,
    ).reshape(row_count, row_count, -1)
    degree = jnp.sum(spectral[:, :, 0], axis=1)
    rounded = spectral.astype(jnp.bfloat16)
    weight_real = jnp.concatenate([rounded[:, :, :half_width], rounded[:, :, :half_width]], axis=2)
    weight_imag = jnp.concatenate([-rounded[:, :, half_width:], rounded[:, :, half_width:]], axis=2)
    filtered = jnp.einsum(
        "ijc,jrc->irc", weight_real, other_block, preferred_element_type=jnp.float32
    )
    filtered = filtered + jnp.einsum(
        "ijc,jrc->irc", weight_imag, swapped, preferred_element_type=jnp.float32
    )
    return (filtered, degree)


def body(coefficients):
    own_block = lax.all_gather(coefficients, "off", axis=1, tiled=True)
    own_inverse = inverse_norms(own_block)
    row_count, radial, angular = own_block.shape
    forward, backward = angle_tables(angular)
    ranges = lax.axis_size("off")
    per_range = min(8, lax.axis_size("blk") // ranges)
    range_index = lax.axis_index("off")
    range_base = range_index * per_range
    packet = own_block
    for bit_number in range(ranges.bit_length() - 1):
        moved_packet = shifted(packet, "blk", -(per_range << bit_number))
        chosen = range_index // (1 << bit_number) % 2 == 1
        packet = jnp.where(chosen, moved_packet, packet)
    empty_sum = jnp.zeros((row_count, radial, angular), jnp.float32)
    empty_degree = jnp.zeros((row_count,), jnp.float32)

    def advance_one(step, loop_state):
        filtered, degree, current = loop_state
        terms = tile_terms(own_block, own_inverse, current, range_base + step, forward, backward)
        current = shifted(current, "blk", -1)
        return (filtered + terms[0], degree + terms[1], current)

    last_step = per_range - 1
    filtered, degree, current = lax.fori_loop(
        0, last_step, advance_one, (empty_sum, empty_degree, packet)
    )
    terms = tile_terms(own_block, own_inverse, current, range_base + last_step, forward, backward)
    filtered = filtered + terms[0]
    degree = degree + terms[1]
    totals = (
        lax.psum_scatter(filtered, "off", scatter_dimension=0, tiled=True),
        lax.psum_scatter(degree, "off", scatter_dimension=0, tiled=True),
    )
    smoothed = totals[0] / totals[1][:, None, None]
    return (smoothed, jnp.log(totals[1]))


def solution(mesh):
    return jax.shard_map(
        body,
        mesh=mesh,
        in_specs=(P("blk", "off", None),),
        out_specs=(P(("blk", "off"), None, None), P(("blk", "off"))),
        check_vma=False,
    )
```

profile of v0, /device:TPU:1, one launch (start us, length us, event | category | flops | bytes accessed | tf_op | source)
XLA Modules:
  0.0 278.7 jit_solution(10738338174467296353)
XLA Ops:
  8.2 28.6 %all_gather.3 = bf16[16,32,128]{0,1,2:T(8,128)(2,1)S(1)} all-gather(bf16[16,8,128]{0,1,2:T(8,128)(2,1)S(1)} %copy.20), channel_id=1, replica_groups=mesh['blk'=128,'off'=4] {'off'}, dimensions={1}, use_global_device_ids=true | all-gather | bytes 163840 | tf_op jit(solution)/shard_map/all_gather | solution.py:74
  38.0 14.6 %collective-permute-start.1 = (bf16[16,32,128]{2,1,0:T(8,128)(2,1)S(1)}, bf16[16,32,128]{2,1,0:T(8,128)(2,1)S(1)}, u32[]{:S(2)}, u32[]{:S(2)}) collective-permute-start(bf16[16,32,128]{2,1,0:T(8,128)(2,1)S(1)} %copy.21), channel_id=1, source_target_pairs={{0,480},{4,484},{8,488},{12,492},{16,496},{20,500},{24,504},{28,50... | collective-permute-start | bytes 393224 | tf_op jit(solution)/shard_map/ppermute | solution.py:13
  53.4 1.9 collective-permute-done.1
  55.3 2.4 copy.22
  60.2 9.7 %collective-permute-start.2 = (bf16[16,32,128]{2,1,0:T(8,128)(2,1)S(1)}, bf16[16,32,128]{2,1,0:T(8,128)(2,1)S(1)}, u32[]{:S(2)}, u32[]{:S(2)}) collective-permute-start(bf16[16,32,128]{2,1,0:T(8,128)(2,1)S(1)} %copy.23), channel_id=1, source_target_pairs={{0,448},{4,452},{8,456},{12,460},{16,464},{20,468},{24,472},{28,47... | collective-permute-start | bytes 393224 | tf_op jit(solution)/shard_map/ppermute | solution.py:13
  71.2 1.8 collective-permute-done.2
  75.6 2.5 copy.25
  78.1 125.4 %while.18 = (s32[]{:T(128)}, f32[16,32,128]{1,0,2:T(8,128)}, f32[16]{0:T(128)}, bf16[16,32,128]{2,1,0:T(8,128)(2,1)S(1)}, bf16[16,32,128]{1,0,2:T(8,128)(2,1)S(1...) while((s32[]{:T(128)}, f32[16,32,128]{1,0,2:T(8,128)}, ...), condition=%wide.region_4.5_spmd.clone, body=%wide.region_1.4_spmd.clone.sunk | while | flops 110216208 | bytes 6230326 | solution.py:97
  78.3 16.1 %collective-permute-start = (bf16[16,32,128]{2,1,0:T(8,128)(2,1)S(1)}, bf16[16,32,128]{2,1,0:T(8,128)(2,1)S(1)}, u32[]{:S(2)}, u32[]{:S(2)}) collective-permute-start(bf16[16,32,128]{2,1,0:T(8,128)(2,1)S(1)} %copy.56), channel_id=1, source_target_pairs={{0,508},{4,0},{8,4},{12,8},{16,12},{20,16},{24,20},{28,24},{32,28}... | collective-permute-start | bytes 393224 | tf_op jit(solution)/shard_map/while/body/eval_jaxpr/ppermute | solution.py:13
  102.4 9.1 %collective-permute-start = (bf16[16,32,128]{2,1,0:T(8,128)(2,1)S(1)}, bf16[16,32,128]{2,1,0:T(8,128)(2,1)S(1)}, u32[]{:S(2)}, u32[]{:S(2)}) collective-permute-start(bf16[16,32,128]{2,1,0:T(8,128)(2,1)S(1)} %copy.56), channel_id=1, source_target_pairs={{0,508},{4,0},{8,4},{12,8},{16,12},{20,16},{24,20},{28,24},{32,28}... | collective-permute-start | bytes 393224 | tf_op jit(solution)/shard_map/while/body/eval_jaxpr/ppermute | solution.py:13
  117.5 2.7 fusion.95
  120.8 7.3 %collective-permute-start = (bf16[16,32,128]{2,1,0:T(8,128)(2,1)S(1)}, bf16[16,32,128]{2,1,0:T(8,128)(2,1)S(1)}, u32[]{:S(2)}, u32[]{:S(2)}) collective-permute-start(bf16[16,32,128]{2,1,0:T(8,128)(2,1)S(1)} %copy.56), channel_id=1, source_target_pairs={{0,508},{4,0},{8,4},{12,8},{16,12},{20,16},{24,20},{28,24},{32,28}... | collective-permute-start | bytes 393224 | tf_op jit(solution)/shard_map/while/body/eval_jaxpr/ppermute | solution.py:13
  134.1 2.7 fusion.95
  137.3 7.3 %collective-permute-start = (bf16[16,32,128]{2,1,0:T(8,128)(2,1)S(1)}, bf16[16,32,128]{2,1,0:T(8,128)(2,1)S(1)}, u32[]{:S(2)}, u32[]{:S(2)}) collective-permute-start(bf16[16,32,128]{2,1,0:T(8,128)(2,1)S(1)} %copy.56), channel_id=1, source_target_pairs={{0,508},{4,0},{8,4},{12,8},{16,12},{20,16},{24,20},{28,24},{32,28}... | collective-permute-start | bytes 393224 | tf_op jit(solution)/shard_map/while/body/eval_jaxpr/ppermute | solution.py:13
  150.6 2.7 fusion.95
  153.9 7.3 %collective-permute-start = (bf16[16,32,128]{2,1,0:T(8,128)(2,1)S(1)}, bf16[16,32,128]{2,1,0:T(8,128)(2,1)S(1)}, u32[]{:S(2)}, u32[]{:S(2)}) collective-permute-start(bf16[16,32,128]{2,1,0:T(8,128)(2,1)S(1)} %copy.56), channel_id=1, source_target_pairs={{0,508},{4,0},{8,4},{12,8},{16,12},{20,16},{24,20},{28,24},{32,28}... | collective-permute-start | bytes 393224 | tf_op jit(solution)/shard_map/while/body/eval_jaxpr/ppermute | solution.py:13
  167.2 2.7 fusion.95
  170.5 7.3 %collective-permute-start = (bf16[16,32,128]{2,1,0:T(8,128)(2,1)S(1)}, bf16[16,32,128]{2,1,0:T(8,128)(2,1)S(1)}, u32[]{:S(2)}, u32[]{:S(2)}) collective-permute-start(bf16[16,32,128]{2,1,0:T(8,128)(2,1)S(1)} %copy.56), channel_id=1, source_target_pairs={{0,508},{4,0},{8,4},{12,8},{16,12},{20,16},{24,20},{28,24},{32,28}... | collective-permute-start | bytes 393224 | tf_op jit(solution)/shard_map/while/body/eval_jaxpr/ppermute | solution.py:13
  183.7 2.7 fusion.95
  187.0 7.3 %collective-permute-start = (bf16[16,32,128]{2,1,0:T(8,128)(2,1)S(1)}, bf16[16,32,128]{2,1,0:T(8,128)(2,1)S(1)}, u32[]{:S(2)}, u32[]{:S(2)}) collective-permute-start(bf16[16,32,128]{2,1,0:T(8,128)(2,1)S(1)} %copy.56), channel_id=1, source_target_pairs={{0,508},{4,0},{8,4},{12,8},{16,12},{20,16},{24,20},{28,24},{32,28}... | collective-permute-start | bytes 393224 | tf_op jit(solution)/shard_map/while/body/eval_jaxpr/ppermute | solution.py:13
  200.3 2.7 fusion.95
  210.1 1.6 fusion.17
  215.0 21.4 %all-reduce = f32[16]{0:T(128)S(1)} all-reduce(f32[16]{0:T(128)S(1)} %add.125), channel_id=3, replica_groups=mesh['blk'=128,'off'=4] {'off'}, use_global_device_ids=true, to_apply=%region_8.9.clone | all-reduce | flops 16 | bytes 128
  237.0 33.3 %reduce-scatter.2.cloned.1.call-done = f32[4,32,128]{2,1,0:T(8,128)} async-done(((f32[16,32,128]{2,1,0:T(8,128)}), f32[4,32,128]{2,1,0:T(8,128)}) %reduce-scatter.2.cloned.1.call-update) | async-done | bytes 65552 | tf_op jit(solution)/shard_map/reduce_scatter | solution.py:104
  (256 shorter events, 66.7 us)
Async XLA Ops:
  7.2 263.1 %reduce-scatter.2.cloned.1.call-start = ((), (), s32[]{:S(2)}) async-start(), calls=%async_computation.1 | async-start | bytes 327680 | tf_op jit(solution)/shard_map/reduce_scatter | solution.py:104
  36.8 33.2 %copy-start = (bf16[16,32,128]{0,1,2:T(8,128)(2,1)}, bf16[16,32,128]{0,1,2:T(8,128)(2,1)S(1)}, u32[]{:S(2)}) copy-start(bf16[16,32,128]{0,1,2:T(8,128)(2,1)S(1)} %all_gather.3) | copy-start | bytes 393220
  38.0 17.3 %collective-permute-start.1 = (bf16[16,32,128]{2,1,0:T(8,128)(2,1)S(1)}, bf16[16,32,128]{2,1,0:T(8,128)(2,1)S(1)}, u32[]{:S(2)}, u32[]{:S(2)}) collective-permute-start(bf16[16,32,128]{2,1,0:T(8,128)(2,1)S(1)} %copy.21), channel_id=1, source_target_pairs={{0,480},{4,484},{8,488},{12,492},{16,496},{20,500},{24,504},{28,50... | collective-permute-start | bytes 393224 | tf_op jit(solution)/shard_map/ppermute | solution.py:13
  53.3 16.6 %copy-start.3 = (f32[64,128]{1,0:T(8,128)}, f32[64,128]{1,0:T(8,128)S(1)}, u32[]{:S(2)}) copy-start(f32[64,128]{1,0:T(8,128)S(1)} %get-tuple-element.249) | copy-start | bytes 98308
  53.3 16.6 %copy-start.5 = (f32[64,128]{1,0:T(8,128)}, f32[64,128]{1,0:T(8,128)S(1)}, u32[]{:S(2)}) copy-start(f32[64,128]{1,0:T(8,128)S(1)} %get-tuple-element.250) | copy-start | bytes 98308
  60.2 12.8 %collective-permute-start.2 = (bf16[16,32,128]{2,1,0:T(8,128)(2,1)S(1)}, bf16[16,32,128]{2,1,0:T(8,128)(2,1)S(1)}, u32[]{:S(2)}, u32[]{:S(2)}) collective-permute-start(bf16[16,32,128]{2,1,0:T(8,128)(2,1)S(1)} %copy.23), channel_id=1, source_target_pairs={{0,448},{4,452},{8,456},{12,460},{16,464},{20,468},{24,472},{28,47... | collective-permute-start | bytes 393224 | tf_op jit(solution)/shard_map/ppermute | solution.py:13
  78.3 23.6 %collective-permute-start = (bf16[16,32,128]{2,1,0:T(8,128)(2,1)S(1)}, bf16[16,32,128]{2,1,0:T(8,128)(2,1)S(1)}, u32[]{:S(2)}, u32[]{:S(2)}) collective-permute-start(bf16[16,32,128]{2,1,0:T(8,128)(2,1)S(1)} %copy.56), channel_id=1, source_target_pairs={{0,508},{4,0},{8,4},{12,8},{16,12},{20,16},{24,20},{28,24},{32,28}... | collective-permute-start | bytes 393224 | tf_op jit(solution)/shard_map/while/body/eval_jaxpr/ppermute | solution.py:13
  100.4 1.5 copy-start.7
  102.4 17.8 %collective-permute-start = (bf16[16,32,128]{2,1,0:T(8,128)(2,1)S(1)}, bf16[16,32,128]{2,1,0:T(8,128)(2,1)S(1)}, u32[]{:S(2)}, u32[]{:S(2)}) collective-permute-start(bf16[16,32,128]{2,1,0:T(8,128)(2,1)S(1)} %copy.56), channel_id=1, source_target_pairs={{0,508},{4,0},{8,4},{12,8},{16,12},{20,16},{24,20},{28,24},{32,28}... | collective-permute-start | bytes 393224 | tf_op jit(solution)/shard_map/while/body/eval_jaxpr/ppermute | solution.py:13
  117.5 2.7 copy-start.7
  120.8 16.0 %collective-permute-start = (bf16[16,32,128]{2,1,0:T(8,128)(2,1)S(1)}, bf16[16,32,128]{2,1,0:T(8,128)(2,1)S(1)}, u32[]{:S(2)}, u32[]{:S(2)}) collective-permute-start(bf16[16,32,128]{2,1,0:T(8,128)(2,1)S(1)} %copy.56), channel_id=1, source_target_pairs={{0,508},{4,0},{8,4},{12,8},{16,12},{20,16},{24,20},{28,24},{32,28}... | collective-permute-start | bytes 393224 | tf_op jit(solution)/shard_map/while/body/eval_jaxpr/ppermute | solution.py:13
  134.1 2.7 copy-start.7
  137.3 16.0 %collective-permute-start = (bf16[16,32,128]{2,1,0:T(8,128)(2,1)S(1)}, bf16[16,32,128]{2,1,0:T(8,128)(2,1)S(1)}, u32[]{:S(2)}, u32[]{:S(2)}) collective-permute-start(bf16[16,32,128]{2,1,0:T(8,128)(2,1)S(1)} %copy.56), channel_id=1, source_target_pairs={{0,508},{4,0},{8,4},{12,8},{16,12},{20,16},{24,20},{28,24},{32,28}... | collective-permute-start | bytes 393224 | tf_op jit(solution)/shard_map/while/body/eval_jaxpr/ppermute | solution.py:13
  150.6 2.7 copy-start.7
  153.9 16.0 %collective-permute-start = (bf16[16,32,128]{2,1,0:T(8,128)(2,1)S(1)}, bf16[16,32,128]{2,1,0:T(8,128)(2,1)S(1)}, u32[]{:S(2)}, u32[]{:S(2)}) collective-permute-start(bf16[16,32,128]{2,1,0:T(8,128)(2,1)S(1)} %copy.56), channel_id=1, source_target_pairs={{0,508},{4,0},{8,4},{12,8},{16,12},{20,16},{24,20},{28,24},{32,28}... | collective-permute-start | bytes 393224 | tf_op jit(solution)/shard_map/while/body/eval_jaxpr/ppermute | solution.py:13
  167.2 2.7 copy-start.7
  170.5 16.0 %collective-permute-start = (bf16[16,32,128]{2,1,0:T(8,128)(2,1)S(1)}, bf16[16,32,128]{2,1,0:T(8,128)(2,1)S(1)}, u32[]{:S(2)}, u32[]{:S(2)}) collective-permute-start(bf16[16,32,128]{2,1,0:T(8,128)(2,1)S(1)} %copy.56), channel_id=1, source_target_pairs={{0,508},{4,0},{8,4},{12,8},{16,12},{20,16},{24,20},{28,24},{32,28}... | collective-permute-start | bytes 393224 | tf_op jit(solution)/shard_map/while/body/eval_jaxpr/ppermute | solution.py:13
  183.7 2.7 copy-start.7
  187.0 16.0 %collective-permute-start = (bf16[16,32,128]{2,1,0:T(8,128)(2,1)S(1)}, bf16[16,32,128]{2,1,0:T(8,128)(2,1)S(1)}, u32[]{:S(2)}, u32[]{:S(2)}) collective-permute-start(bf16[16,32,128]{2,1,0:T(8,128)(2,1)S(1)} %copy.56), channel_id=1, source_target_pairs={{0,508},{4,0},{8,4},{12,8},{16,12},{20,16},{24,20},{28,24},{32,28}... | collective-permute-start | bytes 393224 | tf_op jit(solution)/shard_map/while/body/eval_jaxpr/ppermute | solution.py:13
  200.3 2.7 copy-start.7
  203.7 1.2 copy-start.1
  206.2 0.8 copy-start.6
  208.2 1.9 copy-start.2
  211.7 3.3 %copy-start.9 = (f32[16]{0:T(128)S(1)}, f32[16]{0:T(128)}, u32[]{:S(2)}) copy-start(f32[16]{0:T(128)} %get-tuple-element.160) | copy-start | bytes 196
  (8 other events, 4.8 us)
Sparse Core Ops, SparseCore 0:
  213.0 57.2 reduce-scatter.1
where the time goes:
time: 280 us; the launch traced here: 279 us
  starting transfers between devices  86.1 us (31%)
  blocking collectives  50 us (18%)
  matrix products  40.1 us (14%)
  local copies, waits for them, and re-layouts  37.3 us (13%)
  waiting for transfers between devices  37.1 us (13%)
  between operations  15 us (5%)
  other arithmetic  11.9 us (4%)
    ppermute x9, starting transfers between devices, shifted(): lax.ppermute(array, axis, [(i, (i + by) % count) for i in range(count)])  86.1 us
    reduce_scatter x1, waiting for transfers between devices, body(): lax.psum_scatter(filtered, 'off', scatter_dimension=0, tiled=True)  33.3 us
    all_gather x1, blocking collectives, body(): own_block = lax.all_gather(coefficients, 'off', axis=1, tiled=True)  28.6 us
    unnamed x1, blocking collectives  21.4 us
    dot_general x8, matrix products, tile_terms(): jnp.einsum('ijc,jrc->irc', weight_imag, swapped, preferred_element_type=j...  19.2 us
    dot_general x8, matrix products, tile_terms(): jnp.dot(weights.reshape(row_count * row_count, -1), backward, precision=h...  7.98 us
    while x42, local copies, waits for them, and re-layouts  7.01 us
    unnamed x21, local copies, waits for them, and re-layouts  6.46 us
  transfers between devices with their start and end apart: 10, of which 3 were waited for; matrix products, arithmetic and copies ran while one was open for 22% of the time, Pallas kernels for 0%

commit v1 on v0

--- a/solution.py
+++ b/solution.py
@@ -71,7 +71,8 @@
 
 
 def body(coefficients):
-    own_block = lax.all_gather(coefficients, "off", axis=1, tiled=True)
+    stack = jnp.stack([coefficients] * lax.axis_size("off"))
+    own_block = jnp.concatenate(lax.all_to_all(stack, "off", 0, 0), axis=1)
     own_inverse = inverse_norms(own_block)
     row_count, radial, angular = own_block.shape
     forward, backward = angle_tables(angular)

time: 280 us -> 257 us (0.918)
  blocking collectives: 50 us -> 24.3 us
  starting transfers between devices: 86.1 us -> 96.4 us
  matrix products: 40.1 us -> 31.9 us
  waiting for transfers between devices: 37.1 us -> 44.4 us
  local copies, waits for them, and re-layouts: 37.3 us -> 34.2 us
    all_gather x1 -> x0, blocking collectives: 28.6 us -> none  [body(): own_block = lax.all_gather(coefficients, 'off', axis=1, tiled=True)]
    all_to_all x0 -> x1, starting transfers between devices: none -> 16.6 us  [body(): own_block = jnp.concatenate(lax.all_to_all(stack, 'off', 0, 0), axis=1)]
    all_to_all x0 -> x1, waiting for transfers between devices: none -> 11.6 us  [body(): own_block = jnp.concatenate(lax.all_to_all(stack, 'off', 0, 0), axis=1)]
    ppermute x9, starting transfers between devices: 86.1 us -> 79.9 us  [shifted(): lax.ppermute(array, axis, [(i, (i + by) % count) for i in range(count)])]
    dot_general x8, matrix products: 7.98 us -> 2.1 us  [tile_terms(): jnp.dot(weights.reshape(row_count * row_count, -1), backward, precision=h...]
    reduce_scatter x1, waiting for transfers between devices: 33.3 us -> 29.3 us  [body(): lax.psum_scatter(filtered, 'off', scatter_dimension=0, tiled=True)]
    ppermute x2 -> x0, local copies, waits for them, and re-layouts: 3.87 us -> none  [shifted(): lax.ppermute(array, axis, [(i, (i + by) % count) for i in range(count)])]
    while x42 -> x70, local copies, waits for them, and re-layouts: 7.01 us -> 10.8 us
  transfers between devices with their start and end apart: 10 -> 11, of which waited for: 3 -> 4; matrix products, arithmetic and copies ran while one was open for 22% -> 22% of each run, Pallas kernels for 0% -> 0%
where the time goes in v1:
time: 257 us; the launch traced here: 256 us
  starting transfers between devices  96.4 us (38%)
  waiting for transfers between devices  44.4 us (17%)
  local copies, waits for them, and re-layouts  34.2 us (13%)
  matrix products  31.9 us (12%)
  blocking collectives  24.3 us (9%)
  between operations  15 us (6%)
  other arithmetic  9.26 us (4%)
    ppermute x9, starting transfers between devices, shifted(): lax.ppermute(array, axis, [(i, (i + by) % count) for i in range(count)])  79.9 us
    reduce_scatter x1, waiting for transfers between devices, body(): lax.psum_scatter(filtered, 'off', scatter_dimension=0, tiled=True)  29.3 us
    unnamed x1, blocking collectives  24.3 us
    dot_general x8, matrix products, tile_terms(): jnp.einsum('ijc,jrc->irc', weight_imag, swapped, preferred_element_type=j...  17.8 us
    all_to_all x1, starting transfers between devices, body(): own_block = jnp.concatenate(lax.all_to_all(stack, 'off', 0, 0), axis=1)  16.6 us
    all_to_all x1, waiting for transfers between devices, body(): own_block = jnp.concatenate(lax.all_to_all(stack, 'off', 0, 0), axis=1)  11.6 us
    while x70, local copies, waits for them, and re-layouts  10.8 us
  transfers between devices with their start and end apart: 11, of which 4 were waited for; matrix products, arithmetic and copies ran while one was open for 22% of the time, Pallas kernels for 0%

profile of v1, /device:TPU:1, one launch (start us, length us, event | category | flops | bytes accessed | tf_op | source)
XLA Modules:
  0.0 256.5 jit_solution(16513825102253351620)
XLA Ops:
  7.2 1.4 stack.2
  8.6 16.6 %all-to-all-start = ((bf16[4,16,8,128]{3,2,1,0:T(8,128)(2,1)}), bf16[4,16,8,128]{3,2,1,0:T(8,128)(2,1)S(1)}, u32[]{:S(2)}, u32[]{:S(2)}) async-start(bf16[4,16,8,128]{3,2,1,0:T(8,128)(2,1)} %stack.2), calls=%async_computation | async-start | bytes 262144 | tf_op jit(solution)/shard_map/all_to_all | solution.py:75
  25.9 11.6 %all-to-all-done = bf16[4,16,8,128]{3,2,1,0:T(8,128)(2,1)S(1)} async-done(((bf16[4,16,8,128]{3,2,1,0:T(8,128)(2,1)}), bf16[4,16,8,128]{3,2,1,0:T(8,128)(2,1)S(1)}, u32[]{:S(2)}, u32[]{:S(2)}) %all-to-all-start) | async-done | bytes 131104 | tf_op jit(solution)/shard_map/all_to_all | solution.py:75
  37.6 8.2 %collective-permute-start.1 = (bf16[16,32,128]{2,1,0:T(8,128)(2,1)S(1)}, bf16[16,32,128]{2,1,0:T(8,128)(2,1)S(1)}, u32[]{:S(2)}, u32[]{:S(2)}) collective-permute-start(bf16[16,32,128]{2,1,0:T(8,128)(2,1)S(1)} %bitcast.92), channel_id=1, source_target_pairs={{0,480},{4,484},{8,488},{12,492},{16,496},{20,500},{24,504},{28,50... | collective-permute-start | bytes 393224 | tf_op jit(solution)/shard_map/ppermute | solution.py:13
  47.8 3.7 %collective-permute-start.2 = (bf16[16,32,128]{2,1,0:T(8,128)(2,1)S(1)}, bf16[16,32,128]{2,1,0:T(8,128)(2,1)S(1)}, u32[]{:S(2)}, u32[]{:S(2)}) collective-permute-start(bf16[16,32,128]{2,1,0:T(8,128)(2,1)S(1)} %broadcast_select_fusion.1), channel_id=1, source_target_pairs={{0,448},{4,452},{8,456},{12,460},{16,464},{20,468},{24,472},{28,47... | collective-permute-start | bytes 393224 | tf_op jit(solution)/shard_map/ppermute | solution.py:13
  51.5 2.4 collective-permute-done.2
  53.9 129.3 %while.18 = (s32[]{:T(128)}, f32[16,32,128]{1,0,2:T(8,128)}, f32[16]{0:T(128)}, bf16[16,32,128]{2,1,0:T(8,128)(2,1)S(1)}, bf16[16,32,128]{1,0,2:T(8,128)(2,1)S(1...) while((s32[]{:T(128)}, f32[16,32,128]{1,0,2:T(8,128)}, ...), condition=%wide.region_4.5_spmd.clone, body=%wide.region_1.4_spmd.clone.sunk | while | flops 110216208 | bytes 6754670 | solution.py:98
  54.0 21.0 %collective-permute-start = (bf16[16,32,128]{2,1,0:T(8,128)(2,1)S(1)}, bf16[16,32,128]{2,1,0:T(8,128)(2,1)S(1)}, u32[]{:S(2)}, u32[]{:S(2)}) collective-permute-start(bf16[16,32,128]{2,1,0:T(8,128)(2,1)S(1)} %copy.66), channel_id=1, source_target_pairs={{0,508},{4,0},{8,4},{12,8},{16,12},{20,16},{24,20},{28,24},{32,28}... | collective-permute-start | bytes 393224 | tf_op jit(solution)/shard_map/while/body/eval_jaxpr/ppermute | solution.py:13
  80.1 1.4 fusion.94
  82.6 8.9 %collective-permute-start = (bf16[16,32,128]{2,1,0:T(8,128)(2,1)S(1)}, bf16[16,32,128]{2,1,0:T(8,128)(2,1)S(1)}, u32[]{:S(2)}, u32[]{:S(2)}) collective-permute-start(bf16[16,32,128]{2,1,0:T(8,128)(2,1)S(1)} %copy.66), channel_id=1, source_target_pairs={{0,508},{4,0},{8,4},{12,8},{16,12},{20,16},{24,20},{28,24},{32,28}... | collective-permute-start | bytes 393224 | tf_op jit(solution)/shard_map/while/body/eval_jaxpr/ppermute | solution.py:13
  96.7 2.7 %fusion.94 = f32[16,32,128]{1,0,2:T(8,128)} fusion(f32[16,32,128]{1,0,2:T(8,128)S(1)} %convolution_bitcast_fusion.11, bf16[16,16,128]{1,0,2:T(8,128)(2,1)S(1)} %copy.58, bf16[16,32,128]{1,0,2:T(8,128)(2,1)S(1)} %copy.53, f32[16,32,128]{1,0,2:T(8,128)} %get-tuple-element.347, pred[]{:T(512)S(6)} %compare.9), kind=kOutput, calls=%fused_computation.2.clone.1 | convolution fusion | flops 2293760 | bytes 983041 | tf_op jit(solution)/shard_map/while/body/eval_jaxpr/ijc,jrc->irc/dot_general | solution.py:67
  100.4 7.6 %collective-permute-start = (bf16[16,32,128]{2,1,0:T(8,128)(2,1)S(1)}, bf16[16,32,128]{2,1,0:T(8,128)(2,1)S(1)}, u32[]{:S(2)}, u32[]{:S(2)}) collective-permute-start(bf16[16,32,128]{2,1,0:T(8,128)(2,1)S(1)} %copy.66), channel_id=1, source_target_pairs={{0,508},{4,0},{8,4},{12,8},{16,12},{20,16},{24,20},{28,24},{32,28}... | collective-permute-start | bytes 393224 | tf_op jit(solution)/shard_map/while/body/eval_jaxpr/ppermute | solution.py:13
  113.2 2.7 %fusion.94 = f32[16,32,128]{1,0,2:T(8,128)} fusion(f32[16,32,128]{1,0,2:T(8,128)S(1)} %convolution_bitcast_fusion.11, bf16[16,16,128]{1,0,2:T(8,128)(2,1)S(1)} %copy.58, bf16[16,32,128]{1,0,2:T(8,128)(2,1)S(1)} %copy.53, f32[16,32,128]{1,0,2:T(8,128)} %get-tuple-element.347, pred[]{:T(512)S(6)} %compare.9), kind=kOutput, calls=%fused_computation.2.clone.1 | convolution fusion | flops 2293760 | bytes 983041 | tf_op jit(solution)/shard_map/while/body/eval_jaxpr/ijc,jrc->irc/dot_general | solution.py:67
  117.0 7.6 %collective-permute-start = (bf16[16,32,128]{2,1,0:T(8,128)(2,1)S(1)}, bf16[16,32,128]{2,1,0:T(8,128)(2,1)S(1)}, u32[]{:S(2)}, u32[]{:S(2)}) collective-permute-start(bf16[16,32,128]{2,1,0:T(8,128)(2,1)S(1)} %copy.66), channel_id=1, source_target_pairs={{0,508},{4,0},{8,4},{12,8},{16,12},{20,16},{24,20},{28,24},{32,28}... | collective-permute-start | bytes 393224 | tf_op jit(solution)/shard_map/while/body/eval_jaxpr/ppermute | solution.py:13
  129.8 2.7 %fusion.94 = f32[16,32,128]{1,0,2:T(8,128)} fusion(f32[16,32,128]{1,0,2:T(8,128)S(1)} %convolution_bitcast_fusion.11, bf16[16,16,128]{1,0,2:T(8,128)(2,1)S(1)} %copy.58, bf16[16,32,128]{1,0,2:T(8,128)(2,1)S(1)} %copy.53, f32[16,32,128]{1,0,2:T(8,128)} %get-tuple-element.347, pred[]{:T(512)S(6)} %compare.9), kind=kOutput, calls=%fused_computation.2.clone.1 | convolution fusion | flops 2293760 | bytes 983041 | tf_op jit(solution)/shard_map/while/body/eval_jaxpr/ijc,jrc->irc/dot_general | solution.py:67
  133.6 7.6 %collective-permute-start = (bf16[16,32,128]{2,1,0:T(8,128)(2,1)S(1)}, bf16[16,32,128]{2,1,0:T(8,128)(2,1)S(1)}, u32[]{:S(2)}, u32[]{:S(2)}) collective-permute-start(bf16[16,32,128]{2,1,0:T(8,128)(2,1)S(1)} %copy.66), channel_id=1, source_target_pairs={{0,508},{4,0},{8,4},{12,8},{16,12},{20,16},{24,20},{28,24},{32,28}... | collective-permute-start | bytes 393224 | tf_op jit(solution)/shard_map/while/body/eval_jaxpr/ppermute | solution.py:13
  146.3 2.7 %fusion.94 = f32[16,32,128]{1,0,2:T(8,128)} fusion(f32[16,32,128]{1,0,2:T(8,128)S(1)} %convolution_bitcast_fusion.11, bf16[16,16,128]{1,0,2:T(8,128)(2,1)S(1)} %copy.58, bf16[16,32,128]{1,0,2:T(8,128)(2,1)S(1)} %copy.53, f32[16,32,128]{1,0,2:T(8,128)} %get-tuple-element.347, pred[]{:T(512)S(6)} %compare.9), kind=kOutput, calls=%fused_computation.2.clone.1 | convolution fusion | flops 2293760 | bytes 983041 | tf_op jit(solution)/shard_map/while/body/eval_jaxpr/ijc,jrc->irc/dot_general | solution.py:67
  150.1 7.6 %collective-permute-start = (bf16[16,32,128]{2,1,0:T(8,128)(2,1)S(1)}, bf16[16,32,128]{2,1,0:T(8,128)(2,1)S(1)}, u32[]{:S(2)}, u32[]{:S(2)}) collective-permute-start(bf16[16,32,128]{2,1,0:T(8,128)(2,1)S(1)} %copy.66), channel_id=1, source_target_pairs={{0,508},{4,0},{8,4},{12,8},{16,12},{20,16},{24,20},{28,24},{32,28}... | collective-permute-start | bytes 393224 | tf_op jit(solution)/shard_map/while/body/eval_jaxpr/ppermute | solution.py:13
  162.9 2.7 %fusion.94 = f32[16,32,128]{1,0,2:T(8,128)} fusion(f32[16,32,128]{1,0,2:T(8,128)S(1)} %convolution_bitcast_fusion.11, bf16[16,16,128]{1,0,2:T(8,128)(2,1)S(1)} %copy.58, bf16[16,32,128]{1,0,2:T(8,128)(2,1)S(1)} %copy.53, f32[16,32,128]{1,0,2:T(8,128)} %get-tuple-element.347, pred[]{:T(512)S(6)} %compare.9), kind=kOutput, calls=%fused_computation.2.clone.1 | convolution fusion | flops 2293760 | bytes 983041 | tf_op jit(solution)/shard_map/while/body/eval_jaxpr/ijc,jrc->irc/dot_general | solution.py:67
  166.7 7.6 %collective-permute-start = (bf16[16,32,128]{2,1,0:T(8,128)(2,1)S(1)}, bf16[16,32,128]{2,1,0:T(8,128)(2,1)S(1)}, u32[]{:S(2)}, u32[]{:S(2)}) collective-permute-start(bf16[16,32,128]{2,1,0:T(8,128)(2,1)S(1)} %copy.66), channel_id=1, source_target_pairs={{0,508},{4,0},{8,4},{12,8},{16,12},{20,16},{24,20},{28,24},{32,28}... | collective-permute-start | bytes 393224 | tf_op jit(solution)/shard_map/while/body/eval_jaxpr/ppermute | solution.py:13
  179.4 2.7 %fusion.94 = f32[16,32,128]{1,0,2:T(8,128)} fusion(f32[16,32,128]{1,0,2:T(8,128)S(1)} %convolution_bitcast_fusion.11, bf16[16,16,128]{1,0,2:T(8,128)(2,1)S(1)} %copy.58, bf16[16,32,128]{1,0,2:T(8,128)(2,1)S(1)} %copy.53, f32[16,32,128]{1,0,2:T(8,128)} %get-tuple-element.347, pred[]{:T(512)S(6)} %compare.9), kind=kOutput, calls=%fused_computation.2.clone.1 | convolution fusion | flops 2293760 | bytes 983041 | tf_op jit(solution)/shard_map/while/body/eval_jaxpr/ijc,jrc->irc/dot_general | solution.py:67
  194.0 24.3 %all-reduce = f32[16]{0:T(128)S(1)} all-reduce(f32[16]{0:T(128)S(1)} %add.125), channel_id=3, replica_groups=mesh['blk'=128,'off'=4] {'off'}, use_global_device_ids=true, to_apply=%region_8.9.clone | all-reduce | flops 16 | bytes 128
  218.8 29.3 %reduce-scatter.2.cloned.1.call-done = f32[4,32,128]{2,1,0:T(8,128)} async-done(((f32[16,32,128]{2,1,0:T(8,128)}), f32[4,32,128]{2,1,0:T(8,128)}) %reduce-scatter.2.cloned.1.call-update) | async-done | bytes 65552 | tf_op jit(solution)/shard_map/reduce_scatter | solution.py:105
  248.1 1.5 broadcast_divide_fusion
  (278 shorter events, 56.1 us)
Async XLA Ops:
  8.6 28.9 %all-to-all-start = ((bf16[4,16,8,128]{3,2,1,0:T(8,128)(2,1)}), bf16[4,16,8,128]{3,2,1,0:T(8,128)(2,1)S(1)}, u32[]{:S(2)}, u32[]{:S(2)}) async-start(bf16[4,16,8,128]{3,2,1,0:T(8,128)(2,1)} %stack.2), calls=%async_computation | async-start | bytes 262144 | tf_op jit(solution)/shard_map/all_to_all | solution.py:75
  25.2 222.9 %reduce-scatter.2.cloned.1.call-start = ((), (), s32[]{:S(2)}) async-start(), calls=%async_computation.2 | async-start | bytes 327680 | tf_op jit(solution)/shard_map/reduce_scatter | solution.py:105
  37.6 10.2 %collective-permute-start.1 = (bf16[16,32,128]{2,1,0:T(8,128)(2,1)S(1)}, bf16[16,32,128]{2,1,0:T(8,128)(2,1)S(1)}, u32[]{:S(2)}, u32[]{:S(2)}) collective-permute-start(bf16[16,32,128]{2,1,0:T(8,128)(2,1)S(1)} %bitcast.92), channel_id=1, source_target_pairs={{0,480},{4,484},{8,488},{12,492},{16,496},{20,500},{24,504},{28,50... | collective-permute-start | bytes 393224 | tf_op jit(solution)/shard_map/ppermute | solution.py:13
  47.8 6.1 %collective-permute-start.2 = (bf16[16,32,128]{2,1,0:T(8,128)(2,1)S(1)}, bf16[16,32,128]{2,1,0:T(8,128)(2,1)S(1)}, u32[]{:S(2)}, u32[]{:S(2)}) collective-permute-start(bf16[16,32,128]{2,1,0:T(8,128)(2,1)S(1)} %broadcast_select_fusion.1), channel_id=1, source_target_pairs={{0,448},{4,452},{8,456},{12,460},{16,464},{20,468},{24,472},{28,47... | collective-permute-start | bytes 393224 | tf_op jit(solution)/shard_map/ppermute | solution.py:13
  53.9 24.2 %copy-start.1 = (f32[128,128]{1,0:T(8,128)}, f32[128,128]{1,0:T(8,128)S(1)}, u32[]{:S(2)}) copy-start(f32[128,128]{1,0:T(8,128)S(1)} %get-tuple-element.365) | copy-start | bytes 196612 | tf_op jit(solution)/shard_map/while
  54.0 28.2 %collective-permute-start = (bf16[16,32,128]{2,1,0:T(8,128)(2,1)S(1)}, bf16[16,32,128]{2,1,0:T(8,128)(2,1)S(1)}, u32[]{:S(2)}, u32[]{:S(2)}) collective-permute-start(bf16[16,32,128]{2,1,0:T(8,128)(2,1)S(1)} %copy.66), channel_id=1, source_target_pairs={{0,508},{4,0},{8,4},{12,8},{16,12},{20,16},{24,20},{28,24},{32,28}... | collective-permute-start | bytes 393224 | tf_op jit(solution)/shard_map/while/body/eval_jaxpr/ppermute | solution.py:13
  82.6 12.1 %copy-start.1 = (f32[128,128]{1,0:T(8,128)}, f32[128,128]{1,0:T(8,128)S(1)}, u32[]{:S(2)}) copy-start(f32[128,128]{1,0:T(8,128)S(1)} %get-tuple-element.365) | copy-start | bytes 196612 | tf_op jit(solution)/shard_map/while
  82.6 17.3 %collective-permute-start = (bf16[16,32,128]{2,1,0:T(8,128)(2,1)S(1)}, bf16[16,32,128]{2,1,0:T(8,128)(2,1)S(1)}, u32[]{:S(2)}, u32[]{:S(2)}) collective-permute-start(bf16[16,32,128]{2,1,0:T(8,128)(2,1)S(1)} %copy.66), channel_id=1, source_target_pairs={{0,508},{4,0},{8,4},{12,8},{16,12},{20,16},{24,20},{28,24},{32,28}... | collective-permute-start | bytes 393224 | tf_op jit(solution)/shard_map/while/body/eval_jaxpr/ppermute | solution.py:13
  96.6 3.8 %copy-start.2 = (f32[128,128]{1,0:T(8,128)S(1)}, f32[128,128]{1,0:T(8,128)}, u32[]{:S(2)}) copy-start(f32[128,128]{1,0:T(8,128)} %copy-done.1) | copy-start | bytes 196612 | tf_op jit(solution)/shard_map/while
  100.4 10.8 %copy-start.1 = (f32[128,128]{1,0:T(8,128)}, f32[128,128]{1,0:T(8,128)S(1)}, u32[]{:S(2)}) copy-start(f32[128,128]{1,0:T(8,128)S(1)} %get-tuple-element.365) | copy-start | bytes 196612 | tf_op jit(solution)/shard_map/while
  100.4 16.0 %collective-permute-start = (bf16[16,32,128]{2,1,0:T(8,128)(2,1)S(1)}, bf16[16,32,128]{2,1,0:T(8,128)(2,1)S(1)}, u32[]{:S(2)}, u32[]{:S(2)}) collective-permute-start(bf16[16,32,128]{2,1,0:T(8,128)(2,1)S(1)} %copy.66), channel_id=1, source_target_pairs={{0,508},{4,0},{8,4},{12,8},{16,12},{20,16},{24,20},{28,24},{32,28}... | collective-permute-start | bytes 393224 | tf_op jit(solution)/shard_map/while/body/eval_jaxpr/ppermute | solution.py:13
  113.2 3.8 %copy-start.2 = (f32[128,128]{1,0:T(8,128)S(1)}, f32[128,128]{1,0:T(8,128)}, u32[]{:S(2)}) copy-start(f32[128,128]{1,0:T(8,128)} %copy-done.1) | copy-start | bytes 196612 | tf_op jit(solution)/shard_map/while
  117.0 10.8 %copy-start.1 = (f32[128,128]{1,0:T(8,128)}, f32[128,128]{1,0:T(8,128)S(1)}, u32[]{:S(2)}) copy-start(f32[128,128]{1,0:T(8,128)S(1)} %get-tuple-element.365) | copy-start | bytes 196612 | tf_op jit(solution)/shard_map/while
  117.0 16.0 %collective-permute-start = (bf16[16,32,128]{2,1,0:T(8,128)(2,1)S(1)}, bf16[16,32,128]{2,1,0:T(8,128)(2,1)S(1)}, u32[]{:S(2)}, u32[]{:S(2)}) collective-permute-start(bf16[16,32,128]{2,1,0:T(8,128)(2,1)S(1)} %copy.66), channel_id=1, source_target_pairs={{0,508},{4,0},{8,4},{12,8},{16,12},{20,16},{24,20},{28,24},{32,28}... | collective-permute-start | bytes 393224 | tf_op jit(solution)/shard_map/while/body/eval_jaxpr/ppermute | solution.py:13
  129.8 3.8 %copy-start.2 = (f32[128,128]{1,0:T(8,128)S(1)}, f32[128,128]{1,0:T(8,128)}, u32[]{:S(2)}) copy-start(f32[128,128]{1,0:T(8,128)} %copy-done.1) | copy-start | bytes 196612 | tf_op jit(solution)/shard_map/while
  133.5 10.8 %copy-start.1 = (f32[128,128]{1,0:T(8,128)}, f32[128,128]{1,0:T(8,128)S(1)}, u32[]{:S(2)}) copy-start(f32[128,128]{1,0:T(8,128)S(1)} %get-tuple-element.365) | copy-start | bytes 196612 | tf_op jit(solution)/shard_map/while
  133.6 16.0 %collective-permute-start = (bf16[16,32,128]{2,1,0:T(8,128)(2,1)S(1)}, bf16[16,32,128]{2,1,0:T(8,128)(2,1)S(1)}, u32[]{:S(2)}, u32[]{:S(2)}) collective-permute-start(bf16[16,32,128]{2,1,0:T(8,128)(2,1)S(1)} %copy.66), channel_id=1, source_target_pairs={{0,508},{4,0},{8,4},{12,8},{16,12},{20,16},{24,20},{28,24},{32,28}... | collective-permute-start | bytes 393224 | tf_op jit(solution)/shard_map/while/body/eval_jaxpr/ppermute | solution.py:13
  146.3 3.8 %copy-start.2 = (f32[128,128]{1,0:T(8,128)S(1)}, f32[128,128]{1,0:T(8,128)}, u32[]{:S(2)}) copy-start(f32[128,128]{1,0:T(8,128)} %copy-done.1) | copy-start | bytes 196612 | tf_op jit(solution)/shard_map/while
  150.1 10.8 %copy-start.1 = (f32[128,128]{1,0:T(8,128)}, f32[128,128]{1,0:T(8,128)S(1)}, u32[]{:S(2)}) copy-start(f32[128,128]{1,0:T(8,128)S(1)} %get-tuple-element.365) | copy-start | bytes 196612 | tf_op jit(solution)/shard_map/while
  150.1 16.0 %collective-permute-start = (bf16[16,32,128]{2,1,0:T(8,128)(2,1)S(1)}, bf16[16,32,128]{2,1,0:T(8,128)(2,1)S(1)}, u32[]{:S(2)}, u32[]{:S(2)}) collective-permute-start(bf16[16,32,128]{2,1,0:T(8,128)(2,1)S(1)} %copy.66), channel_id=1, source_target_pairs={{0,508},{4,0},{8,4},{12,8},{16,12},{20,16},{24,20},{28,24},{32,28}... | collective-permute-start | bytes 393224 | tf_op jit(solution)/shard_map/while/body/eval_jaxpr/ppermute | solution.py:13
  162.9 3.8 %copy-start.2 = (f32[128,128]{1,0:T(8,128)S(1)}, f32[128,128]{1,0:T(8,128)}, u32[]{:S(2)}) copy-start(f32[128,128]{1,0:T(8,128)} %copy-done.1) | copy-start | bytes 196612 | tf_op jit(solution)/shard_map/while
  166.7 10.8 %copy-start.1 = (f32[128,128]{1,0:T(8,128)}, f32[128,128]{1,0:T(8,128)S(1)}, u32[]{:S(2)}) copy-start(f32[128,128]{1,0:T(8,128)S(1)} %get-tuple-element.365) | copy-start | bytes 196612 | tf_op jit(solution)/shard_map/while
  166.7 16.0 %collective-permute-start = (bf16[16,32,128]{2,1,0:T(8,128)(2,1)S(1)}, bf16[16,32,128]{2,1,0:T(8,128)(2,1)S(1)}, u32[]{:S(2)}, u32[]{:S(2)}) collective-permute-start(bf16[16,32,128]{2,1,0:T(8,128)(2,1)S(1)} %copy.66), channel_id=1, source_target_pairs={{0,508},{4,0},{8,4},{12,8},{16,12},{20,16},{24,20},{28,24},{32,28}... | collective-permute-start | bytes 393224 | tf_op jit(solution)/shard_map/while/body/eval_jaxpr/ppermute | solution.py:13
  179.4 3.8 %copy-start.2 = (f32[128,128]{1,0:T(8,128)S(1)}, f32[128,128]{1,0:T(8,128)}, u32[]{:S(2)}) copy-start(f32[128,128]{1,0:T(8,128)} %copy-done.1) | copy-start | bytes 196612 | tf_op jit(solution)/shard_map/while
  (21 other events, 14.8 us)
Sparse Core Ops, SparseCore 0:
  191.4 56.7 reduce-scatter.1
